TPU v7x, 1024 devices: a whole 4x8x16 slice. The times are simulated.
1024 devices in a mesh: section: 16 (over x, y_hi), hid: 64 (over y_lo, z, core).
Axes of the slice: x: 4, y: 8 (y_hi: 4, y_lo: 2; y = y_hi * 2 + y_lo), z: 16, core: 2. Of those that a mesh axis runs over, the one named last changes fastest.
Arguments:
- layer_input: bfloat16 [16, 256, 4096], P('section', 'hid'), may hold values from -6 to 6
- hidden_grad: bfloat16 [16, 128, 7168], P('section', None, 'hid'), may hold values from -3 to 3
- gate_weight: bfloat16 [16, 4096, 7168], P('section', None, 'hid'), may hold values from -0.09375 to 0.09375
- up_weight: bfloat16 [16, 4096, 7168], P('section', None, 'hid'), may hold values from -0.09375 to 0.09375
- expert_ids: int32 [16, 256, 2], replicated, may hold values from 0 to 7, as said below
Outputs:
- grad_in: bfloat16 [16, 256, 4096], P('section', 'hid')
- grad_gate_weight: bfloat16 [16, 4096, 7168], P('section', None, 'hid')
Inputs may be any that keep to these rules, and one draw needn't show every extreme that they name: `expert_ids`: each token names two different experts. In every aligned block of 4 tokens of one section, between 1 and 2 tokens name expert 0; in one section every block has exactly 2.
All inputs are finite; a program needn't handle non-finite values.
Results may differ from a plain program's by a relative error of at most 0.0049.
Values may be sent and summed in bfloat16 or wider, within the bound.
A program may use at most 32 MiB of HBM per device.

v0:
```python
import jax
import jax.numpy as jnp
from jax import lax
from jax.sharding import PartitionSpec as P


def shifted(value, axis, steps):
    count = lax.axis_size(axis)
    pairs = [(source, (source + steps) % count) for source in range(count)]
    return lax.ppermute(value, axis, pairs)


def own_table(ids, hid_at, tok_dev, k_dev):
    chosen = jnp.any(ids == 0, axis=1).astype(jnp.int32)
    local = lax.dynamic_slice_in_dim(chosen, hid_at * tok_dev, tok_dev, 0)
    slot_rank = jnp.cumsum(local) - local
    slot_iota = lax.broadcasted_iota(jnp.int32, (k_dev, tok_dev), 0)
    matches = (slot_rank[None, :] == slot_iota) & (local[None, :] == 1)
    return matches.astype(jnp.bfloat16)


def contract_last(left, right):
    return lax.dot_general(
        left, right, (((1,), (1,)), ((), ())), preferred_element_type=jnp.float32
    )


def contract_first(left, right):
    return lax.dot_general(
        left, right, (((0,), (0,)), ((), ())), preferred_element_type=jnp.float32
    )


def per_device(layer_input, hidden_grad, gate_weight, up_weight, expert_ids):
    tok_dev = layer_input.shape[1]
    k_dev = tok_dev // 2
    section_at = lax.axis_index("section")
    hid_at = lax.axis_index("hid")
    section_ids = lax.dynamic_index_in_dim(expert_ids, section_at, 0, keepdims=False)
    table = own_table(section_ids, hid_at, tok_dev, k_dev)
    packed = jnp.dot(table, layer_input[0], preferred_element_type=jnp.float32).astype(jnp.bfloat16)
    slot_rows = lax.all_gather(packed, "hid", axis=0, tiled=True)
    gate_local = gate_weight[0]
    up_local = up_weight[0]
    gate_act = jnp.dot(slot_rows, gate_local, preferred_element_type=jnp.float32)
    up_act = jnp.dot(slot_rows, up_local, preferred_element_type=jnp.float32)
    sigmoid_gate = jax.nn.sigmoid(gate_act)
    hidden_float = hidden_grad[0].astype(jnp.float32)
    grad_gate_act = (
        hidden_float * up_act * sigmoid_gate * (1.0 + gate_act * (1.0 - sigmoid_gate))
    ).astype(jnp.bfloat16)
    grad_up_act = (hidden_float * gate_act * sigmoid_gate).astype(jnp.bfloat16)
    summed = lax.psum_scatter(
        contract_last(grad_gate_act, gate_local) + contract_last(grad_up_act, up_local),
        "hid",
        scatter_dimension=0,
        tiled=True,
    )
    own_grad = summed.astype(jnp.bfloat16)
    token_grad = contract_first(table, own_grad).astype(jnp.bfloat16)
    passed = shifted(token_grad, "section", -1)
    weight_grad = contract_first(slot_rows, grad_gate_act).astype(jnp.bfloat16)
    return (passed[None], weight_grad[None])


def solution(mesh):
    return jax.shard_map(
        per_device,
        mesh=mesh,
        in_specs=(
            P("section", "hid", None),
            P("section", None, "hid"),
            P("section", None, "hid"),
            P("section", None, "hid"),
            P(),
        ),
        out_specs=(P("section", "hid", None), P("section", None, "hid")),
        check_vma=False,
    )
```

profile of v0, /device:TPU:62, one launch (start us, length us, event | category | flops | bytes accessed | tf_op | source)
XLA Modules:
  0.0 396.1 jit_solution(14920024062110310564)
XLA Ops:
  7.2 0.0 copy-start
  7.2 0.0 all-gather.3.cloned.1.call-start
  7.2 0.8 compare_reduce_fusion
  8.0 0.1 broadcast_compare_fusion
  8.1 0.1 dynamic-slice_bitcast_fusion
  8.2 0.2 reduce-window.9
  8.3 0.1 bitcast_subtract_fusion
  8.4 1.5 fusion.1
  9.9 0.0 copy-start.1
  9.9 0.0 copy-start.2
  9.9 0.0 all-gather.3.cloned.1.call-update
  10.0 1.3 dynamic-slice
  12.0 130.8 %all-gather.3.cloned.1.call-done = bf16[64,2,4096]{2,1,0:T(2,128)(2,1)} async-done(((bf16[1,2,4096]{2,1,0:T(2,128)(2,1)}), bf16[64,2,4096]{2,1,0:T(2,128)(2,1)}) %all-gather.3.cloned.1.call-update) | async-done | bytes 1048592 | tf_op jit(solution)/shard_map/all_gather | solution.py:42
  142.7 1.5 reshape.41
  144.2 0.0 copy-done
  144.2 0.4 fusion.7
  144.7 0.0 copy-done.1
  144.7 0.0 copy-done.2
  144.7 0.5 fusion.4
  145.1 0.5 fusion.5
  145.6 1.8 convolution_add_fusion
  147.4 231.0 %all-reduce.2 = bf16[128,4096]{1,0:T(8,128)(2,1)S(1)} all-reduce(f32[128,4096]{1,0:T(8,128)} %convolution_add_fusion), channel_id=2, replica_groups=mesh['section'=16,'hid'=64] {'hid'}, use_global_device_ids=true, to_apply=%region_2.3.clone | all-reduce | flops 524288 | bytes 3145728
  378.4 0.2 convolution_convert_fusion.1
  378.6 4.2 %collective-permute-start = (bf16[4,4096]{1,0:T(4,128)(2,1)S(1)}, bf16[4,4096]{1,0:T(4,128)(2,1)S(1)}, u32[]{:S(2)}, u32[]{:S(2)}) collective-permute-start(bf16[4,4096]{1,0:T(4,128)(2,1)S(1)} %convolution_convert_fusion.1), channel_id=1, source_target_pairs={{0,960},{64,0},{128,64},{192,128},{256,192},{320,256},{384,320},{4... | collective-permute-start | bytes 98312 | tf_op jit(solution)/shard_map/ppermute | solution.py:10
  382.9 1.3 fusion
  384.2 4.5 %collective-permute-done = bf16[4,4096]{1,0:T(4,128)(2,1)S(1)} collective-permute-done((bf16[4,4096]{1,0:T(4,128)(2,1)S(1)}, bf16[4,4096]{1,0:T(4,128)(2,1)S(1)}, u32[]{:S(2)}, u32[]{:S(2)}) %collective-permute-start) | collective-permute-done | bytes 32800 | tf_op jit(solution)/shard_map/ppermute | solution.py:10
  388.6 0.6 copy.10
  (1 shorter events, 0.0 us)
Async XLA Ops:
  7.2 137.0 %copy-start = (bf16[1,4096,112]{1,2,0:T(8,128)(2,1)S(1)}, bf16[1,4096,112]{1,2,0:T(8,128)(2,1)}, u32[]{:S(2)}) copy-start(bf16[1,4096,112]{1,2,0:T(8,128)(2,1)} %param.7) | copy-start | bytes 2752516
  7.2 135.6 %all-gather.3.cloned.1.call-start = ((), (), s32[]{:S(2)}) async-start(), calls=%async_computation | async-start | bytes 1064960 | tf_op jit(solution)/shard_map/all_gather | solution.py:42
  9.9 134.7 %copy-start.1 = (bf16[1,4096,112]{1,2,0:T(8,128)(2,1)S(1)}, bf16[1,4096,112]{1,2,0:T(8,128)(2,1)}, u32[]{:S(2)}) copy-start(bf16[1,4096,112]{1,2,0:T(8,128)(2,1)} %param.8) | copy-start | bytes 2752516
  9.9 134.7 %copy-start.2 = (bf16[1,128,112]{1,2,0:T(8,128)(2,1)S(1)}, bf16[1,128,112]{1,2,0:T(8,128)(2,1)}, u32[]{:S(2)}) copy-start(bf16[1,128,112]{1,2,0:T(8,128)(2,1)} %param.6) | copy-start | bytes 86020
  378.6 10.0 %collective-permute-start = (bf16[4,4096]{1,0:T(4,128)(2,1)S(1)}, bf16[4,4096]{1,0:T(4,128)(2,1)S(1)}, u32[]{:S(2)}, u32[]{:S(2)}) collective-permute-start(bf16[4,4096]{1,0:T(4,128)(2,1)S(1)} %convolution_convert_fusion.1), channel_id=1, source_target_pairs={{0,960},{64,0},{128,64},{192,128},{256,192},{320,256},{384,320},{4... | collective-permute-start | bytes 98312 | tf_op jit(solution)/shard_map/ppermute | solution.py:10
Sparse Core Ops, SparseCore 0:
  11.3 131.3 all-gather.2
where the time goes:
time: 396 us
  blocking collectives  231 us (58%)
  waiting for transfers between devices  135 us (34%)
  between operations  14.8 us (4%)
  matrix products  6.22 us (2%)
  starting transfers between devices  4.27 us (1%)
    unnamed x1, blocking collectives  231 us
    all_gather x1, waiting for transfers between devices, per_device(): slot_rows = lax.all_gather(packed, 'hid', axis=0, tiled=True)  131 us
  transfers between devices with their start and end apart: 2, of which 2 were waited for; matrix products, arithmetic and copies ran while one was open for 1% of the time, Pallas kernels for 0%

commit v1 on v0

v1 whole, which is shorter than its diff:
```python
import functools

import jax
import jax.numpy as jnp
from jax import lax
from jax.experimental import pallas as pl
from jax.experimental.pallas import tpu as pltpu
from jax.sharding import PartitionSpec as P

MESH = pl.DeviceIdType.MESH
F32 = jnp.float32
BF16 = jnp.bfloat16
Z = 16
ZZ = Z // 2
D = 4096
CH = 8
CW = D // CH
FL = 112


def nt(left, right):
    return lax.dot_general(left, right, (((1,), (1,)), ((), ())), preferred_element_type=F32)


def nn(left, right):
    return lax.dot_general(left, right, (((1,), (0,)), ((), ())), preferred_element_type=F32)


def tn(left, right):
    return lax.dot_general(left, right, (((0,), (0,)), ((), ())), preferred_element_type=F32)


def iota(shape, dim):
    return lax.broadcasted_iota(jnp.int32, shape, dim)


def one_hot(mask):
    return jnp.where(mask, 1.0, 0.0).astype(BF16)


def piece_to_block(i):
    return (i % 8) * 16 + (i // 16) * 2 + (i // 8) % 2


def slots_of(ids_ref, hid_at):
    taken = jnp.int32(0)
    slots = []
    for t in range(4):
        chosen = jnp.where(ids_ref[0, hid_at * 4 + t] * ids_ref[1, hid_at * 4 + t] == 0, 1, 0)
        slots.append(jnp.where(chosen == 1, taken, -1))
        taken = taken + chosen
    return slots


def kernel(
    x_hbm, h_hbm, wg_hbm, wu_hbm, ids_hbm, out_ref, wgrad_hbm,
    xs, hs, wg, wu, ids_a, ids_b, far, rows, hid, gg, part, wgrad,
    s1, r1, s2, r2, s3, r3, s4, r4, s5, r5,
    load_sem, out_sem,
    farg_s, farg_r, nearg_s, nearg_r, yg_s, yg_r, cg_s, cg_r,
    c_s, c_r, y_s, y_r, near_s, near_r, far_s, far_r, pass_s, pass_r,
):
    sec = lax.axis_index("section")
    n_sec = lax.axis_size("section")
    me = lax.axis_index("hid")
    core = me % 2
    z = (me // 2) % Z
    y = me // (2 * Z)
    zz = z // 2
    par = z % 2
    prev_sec = (sec + n_sec - 1) % n_sec
    next_sec = (sec + 1) % n_sec

    def hid_of(y_at, z_at, core_at):
        return (y_at * Z + z_at) * 2 + core_at

    up_z = hid_of(y, (z + 1) % Z, core)
    down_z = hid_of(y, (z + Z - 1) % Z, core)
    other_y = hid_of(1 - y, z, core)
    other_core = hid_of(y, z, 1 - core)
    far_z = [hid_of(y, (z + 2 * k) % Z, core) for k in range(ZZ)]

    def loads(src, dst, i):
        return pltpu.make_async_copy(src, dst, load_sem.at[i])

    def remote(src, dst, send, recv, to, section=None):
        return pltpu.make_async_remote_copy(
            src_ref=src, dst_ref=dst, send_sem=send, recv_sem=recv,
            device_id={"section": sec if section is None else section, "hid": to},
            device_id_type=MESH,
        )

    load_ids = loads(ids_hbm.at[sec], ids_a, 0)
    load_next = loads(ids_hbm.at[next_sec], ids_b, 1)
    load_x = loads(x_hbm.at[0], xs, 2)
    load_h = loads(h_hbm, hs, 3)
    load_wg = loads(wg_hbm, wg, 4)
    load_wu = loads(wu_hbm, wu, 5)
    for c in (load_ids, load_x, load_next, load_h, load_wg, load_wu):
        c.start()

    barrier = pltpu.get_barrier_semaphore()
    peers = far_z[1:] + [up_z, down_z, other_y, other_core]
    for p in peers:
        pl.semaphore_signal(barrier, inc=1, device_id={"section": sec, "hid": p}, device_id_type=MESH)
    pl.semaphore_signal(barrier, inc=1, device_id={"section": next_sec, "hid": me}, device_id_type=MESH)

    load_ids.wait()
    load_x.wait()
    slots = slots_of(ids_a, me)
    row, tok = iota((16, 4), 0), iota((16, 4), 1)
    slot_of_tok = jnp.full((16, 4), -1, jnp.int32)
    for t in range(4):
        slot_of_tok = jnp.where(tok == t, slots[t], slot_of_tok)
    tok_rows = xs[...]
    piece = jnp.zeros((16, CW), F32)
    for j in range(CH):
        pick = one_hot((row // 8 == slot_of_tok) & (row % 8 == j))
        piece += nn(pick, tok_rows[:, j * CW:(j + 1) * CW])
    far[zz] = piece.astype(BF16)

    pl.semaphore_wait(barrier, len(peers) + 1)

    sends = []

    def send(*a, **k):
        c = remote(*a, **k)
        c.start()
        sends.append(c)
        return c

    order = sorted(range(1, ZZ), key=lambda k: -min(k, ZZ - k))
    for k in order:
        send(far.at[zz], far.at[zz], farg_s.at[k - 1], farg_r.at[k - 1], far_z[k])

    load_h.wait()
    m, o = iota((128, 128), 0), iota((128, 128), 1)
    slot_at = ((m // 32) % 2) * 64 + ((m // 2) % 8) * 8 + ((m // 16) % 2) * 4 + (m // 64) * 2 + m % 2
    hid[...] = nt(one_hot(o == slot_at), hs[...]).reshape(4, 32, FL)
    load_wg.wait()
    load_wu.wait()

    for k in order:
        src = (zz + ZZ - k) % ZZ
        remote(far.at[src], far.at[src], farg_s.at[k - 1], farg_r.at[k - 1], far_z[k]).wait_recv()
    to_block = one_hot(m == piece_to_block(o))
    moved = nn(to_block, far[...].reshape(128, CW)).astype(BF16)
    blk = (core * 2 + y) * 2 + par
    blk_p = (core * 2 + y) * 2 + 1 - par
    for j in range(CH):
        rows[blk, :, j * CW:(j + 1) * CW] = moved[j * 16:(j + 1) * 16]

    half = D // 2
    for i, to in ((0, up_z), (1, down_z)):
        cols = pl.ds(i * half, half)
        send(rows.at[blk, :, cols], rows.at[blk, :, cols], nearg_s.at[i], nearg_r.at[i], to)
    send(rows.at[blk], rows.at[blk], yg_s.at[0], yg_r.at[0], other_y)
    send(rows.at[blk], rows.at[blk], cg_s.at[0], cg_r.at[0], other_core)
    for i, to in ((0, up_z), (1, down_z)):
        cols = pl.ds(i * half, half)
        remote(rows.at[blk_p, :, cols], rows.at[blk_p, :, cols], nearg_s.at[i], nearg_r.at[i], to).wait_recv()
    send(rows.at[blk_p], rows.at[blk_p], yg_s.at[1], yg_r.at[1], other_y)
    send(rows.at[blk_p], rows.at[blk_p], cg_s.at[1], cg_r.at[1], other_core)

    def group(core_at, y_at):
        g = core_at * 2 + y_at
        xg = rows[pl.ds(g * 2, 2)].reshape(32, D)
        gate = nt(xg, wg[...])
        up = nt(xg, wu[...])
        sig = 1.0 / (1.0 + jnp.exp(-gate))
        hf = hid[g]
        d_gate = (hf * up * sig * (1.0 + gate * (1.0 - sig))).astype(BF16)
        d_up = (hf * gate * sig).astype(BF16)
        gg[g] = d_gate
        part[pl.ds(g * 2, 2)] = (nn(d_gate, wg[...]) + nn(d_up, wu[...])).reshape(2, 16, D)

    group(core, y)
    yblk = (core * 2 + 1 - y) * 2 + par
    yblk_p = (core * 2 + 1 - y) * 2 + 1 - par
    remote(rows.at[yblk], rows.at[yblk], yg_s.at[0], yg_r.at[0], other_y).wait_recv()
    send(rows.at[yblk], rows.at[yblk], cg_s.at[2], cg_r.at[2], other_core)
    remote(rows.at[yblk_p], rows.at[yblk_p], yg_s.at[1], yg_r.at[1], other_y).wait_recv()
    send(rows.at[yblk_p], rows.at[yblk_p], cg_s.at[3], cg_r.at[3], other_core)

    def from_core(i, y_at, par_at):
        b = ((1 - core) * 2 + y_at) * 2 + par_at
        remote(rows.at[b], rows.at[b], cg_s.at[i], cg_r.at[i], other_core).wait_recv()

    def to_core(i, y_at, par_at):
        b = ((1 - core) * 2 + y_at) * 2 + par_at
        s1[i] = part[b].astype(BF16)
        send(s1.at[i], r1.at[i], c_s.at[i], c_r.at[i], other_core)

    group(core, 1 - y)
    from_core(0, y, par)
    from_core(1, y, 1 - par)
    group(1 - core, y)
    from_core(2, 1 - y, par)
    from_core(3, 1 - y, 1 - par)
    group(1 - core, 1 - y)
    to_core(0, 1 - y, 1 - par)
    to_core(1, 1 - y, par)
    to_core(2, y, 1 - par)
    to_core(3, y, par)

    def core_sum(i, y_at, par_at):
        remote(s1.at[i], r1.at[i], c_s.at[i], c_r.at[i], other_core).wait_recv()
        b = (core * 2 + y_at) * 2 + par_at
        return part[b] + r1[i].astype(F32)

    for i, par_at in ((0, 1 - par), (1, par)):
        s2[i] = core_sum(i, 1 - y, par_at).astype(BF16)
        send(s2.at[i], r2.at[i], y_s.at[i], y_r.at[i], other_y)
    part[blk_p] = core_sum(2, y, 1 - par)
    part[blk] = core_sum(3, y, par)

    all_gg = gg[...].reshape(128, FL)
    for j in range(CH):
        cols = slice(j * CW, (j + 1) * CW)
        wgrad[:, cols] = tn(all_gg, rows[:, :, cols].reshape(128, CW)).astype(BF16)
    store = pltpu.make_async_copy(wgrad, wgrad_hbm, out_sem)
    store.start()

    remote(s2.at[0], r2.at[0], y_s.at[0], y_r.at[0], other_y).wait_recv()
    s3[...] = (part[blk_p] + r2[0].astype(F32)).astype(BF16)
    for i, to in ((0, up_z), (1, down_z)):
        cols = pl.ds(i * half, half)
        send(s3.at[:, cols], r3.at[:, cols], near_s.at[i], near_r.at[i], to)
    remote(s2.at[1], r2.at[1], y_s.at[1], y_r.at[1], other_y).wait_recv()
    own = part[blk] + r2[1].astype(F32)
    for i, to in ((0, up_z), (1, down_z)):
        cols = pl.ds(i * half, half)
        remote(s3.at[:, cols], r3.at[:, cols], near_s.at[i], near_r.at[i], to).wait_recv()
    own = (own + r3[...].astype(F32)).astype(BF16)
    to_piece = one_hot(o == piece_to_block(m))
    stacked = jnp.concatenate([own[:, j * CW:(j + 1) * CW] for j in range(CH)], axis=0)
    s4[...] = nn(to_piece, stacked).astype(BF16).reshape(ZZ, 16, CW)
    for k in order:
        to = (zz + k) % ZZ
        send(s4.at[to], r4.at[k - 1], far_s.at[k - 1], far_r.at[k - 1], far_z[k])
    total = s4[zz].astype(F32)
    for k in order:
        remote(s4.at[zz], r4.at[k - 1], far_s.at[k - 1], far_r.at[k - 1], far_z[k]).wait_recv()
        total += r4[k - 1].astype(F32)
    s5[...] = total.astype(BF16)
    send(s5, r5, pass_s, pass_r, me, section=prev_sec)

    load_next.wait()
    slots_n = slots_of(ids_b, me)
    trow, tcol = iota((4, 16), 0), iota((4, 16), 1)
    slot_of_row = jnp.full((4, 16), -1, jnp.int32)
    for t in range(4):
        slot_of_row = jnp.where(trow == t, slots_n[t], slot_of_row)
    store.wait()
    for c in sends[:-1]:
        c.wait_send()
    sends[-1].wait()
    got = r5[...]
    for j in range(CH):
        pick = one_hot((tcol // 8 == slot_of_row) & (tcol % 8 == j))
        out_ref[0, :, j * CW:(j + 1) * CW] = nn(pick, got).astype(BF16)


def per_device(layer_input, hidden_grad, gate_weight, up_weight, expert_ids):
    dma = pltpu.SemaphoreType.DMA
    anywhere = pl.BlockSpec(memory_space=pl.ANY)
    out, wgrad = pl.pallas_call(
        kernel,
        out_shape=(
            jax.ShapeDtypeStruct((1, 4, D), BF16),
            jax.ShapeDtypeStruct((FL, D), BF16),
        ),
        in_specs=[anywhere] * 5,
        out_specs=(pl.BlockSpec(memory_space=pltpu.VMEM), anywhere),
        scratch_shapes=[
            pltpu.VMEM((4, D), BF16),
            pltpu.VMEM((FL, 128), BF16),
            pltpu.VMEM((FL, D), BF16),
            pltpu.VMEM((FL, D), BF16),
            pltpu.SMEM((2, 256), jnp.int32),
            pltpu.SMEM((2, 256), jnp.int32),
            pltpu.VMEM((ZZ, 16, CW), BF16),
            pltpu.VMEM((8, 16, D), BF16),
            pltpu.VMEM((4, 32, FL), F32),
            pltpu.VMEM((4, 32, FL), BF16),
            pltpu.VMEM((8, 16, D), F32),
            pltpu.VMEM((FL, D), BF16),
            pltpu.VMEM((4, 16, D), BF16),
            pltpu.VMEM((4, 16, D), BF16),
            pltpu.VMEM((2, 16, D), BF16),
            pltpu.VMEM((2, 16, D), BF16),
            pltpu.VMEM((16, D), BF16),
            pltpu.VMEM((16, D), BF16),
            pltpu.VMEM((ZZ, 16, CW), BF16),
            pltpu.VMEM((ZZ - 1, 16, CW), BF16),
            pltpu.VMEM((16, CW), BF16),
            pltpu.VMEM((16, CW), BF16),
            dma((6,)),
            dma,
            dma((ZZ - 1,)), dma((ZZ - 1,)),
            dma((2,)), dma((2,)),
            dma((2,)), dma((2,)),
            dma((4,)), dma((4,)),
            dma((4,)), dma((4,)),
            dma((2,)), dma((2,)),
            dma((2,)), dma((2,)),
            dma((ZZ - 1,)), dma((ZZ - 1,)),
            dma, dma,
        ],
        compiler_params=pltpu.CompilerParams(
            collective_id=0, has_side_effects=True, vmem_limit_bytes=60 * 2**20
        ),
        name="relay",
    )(
        layer_input,
        jnp.swapaxes(hidden_grad[0], 0, 1),
        jnp.swapaxes(gate_weight[0], 0, 1),
        jnp.swapaxes(up_weight[0], 0, 1),
        jnp.swapaxes(expert_ids, 1, 2),
    )
    return out, jnp.swapaxes(wgrad, 0, 1)[None]


def solution(mesh):
    return jax.shard_map(
        per_device,
        mesh=mesh,
        in_specs=(
            P("section", "hid", None),
            P("section", None, "hid"),
            P("section", None, "hid"),
            P("section", None, "hid"),
            P(),
        ),
        out_specs=(P("section", "hid", None), P("section", None, "hid")),
        check_vma=False,
    )
```

time: 396 us -> 70.2 us (0.18)
  the two profiles are of different devices: /device:TPU:62 before, /device:TPU:18 now
where the time goes in v1:
time: 70.2 us; the launch traced here: 69.9 us
  Pallas kernels  65.8 us (94%)
  local copies, waits for them, and re-layouts  3.55 us (5%)
    pallas_call x1, Pallas kernels, per_device(): pl.pallas_call(kernel, out_shape=(jax.ShapeDtypeStruct((1, 4, D), BF16),...  65.8 us
    unnamed x2, local copies, waits for them, and re-layouts  3.55 us

profile of v1, /device:TPU:18, one launch (start us, length us, event | category | flops | bytes accessed | tf_op | source)
XLA Modules:
  0.0 69.9 jit_solution(8387928981840883108)
XLA Ops:
  0.6 65.8 %relay.1 = (bf16[1,4,4096]{2,1,0:T(4,128)(2,1)}, bf16[112,4096]{1,0:T(8,128)(2,1)}) custom-call(bf16[1,4,4096]{2,1,0:T(4,128)(2,1)} %x_hbm.1, bf16[112,128]{1,0:T(8,128)(2,1)} %bitcast.17, bf16[112,4096]{1,0:T(8,128)(2,1)} %bitcast.14, bf16[112,4096]{1,0:T(8,128)(2,1)} %bitcast.15, s32[16,2,256]{2,1,0:T(2,128)} %bitcast.16), custom_call_target="tpu_custom_call" | custom-call | tf_op jit(solution)/shard_map/relay/pallas_call | solution.py:267
  66.4 1.4 %copy.9 = bf16[1,4,4096]{2,1,0:T(4,128)(2,1)} copy(bf16[1,4,4096]{2,1,0:T(4,128)(2,1)} %get-tuple-element.8) | data formatting | bytes 65536
  67.8 2.2 %copy.10 = bf16[1,4096,112]{1,2,0:T(8,128)(2,1)} copy(bf16[1,4096,112]{1,2,0:T(8,128)(2,1)} %bitcast.13) | data formatting | bytes 1835008

commit v2 on v1

v2 whole, which is shorter than its diff:
```python
import functools

import jax
import jax.numpy as jnp
from jax import lax
from jax.experimental import pallas as pl
from jax.experimental.pallas import tpu as pltpu
from jax.sharding import PartitionSpec as P

MESH = pl.DeviceIdType.MESH
F32 = jnp.float32
BF16 = jnp.bfloat16
Z = 16
D = 4096
CH = 8
CW = D // CH
FL = 112

DISTANCES = tuple(range(1 - Z // 2, Z // 2 + 1))
FIRST, EACH, Y_TRIP, SLOT = 1.4, 0.6, 2.1, 0.28


def both_ways(tree):
    back = {-d: -p for d, p in tree.items() if d < Z // 2}
    return {**tree, **back}


GATHER_FROM = both_ways({1: 0, 2: 1, 3: 2, 4: 0, 5: 4, 6: 4, 7: 4, 8: 4})
SUM_FROM = both_ways({1: 0, 2: 0, 3: 0, 4: 0, 5: 4, 6: 2, 7: 4, 8: 4})


def trip(tree, d):
    return 0.0 if d == 0 else FIRST + EACH * abs(d - tree[d]) + trip(tree, tree[d])


def below(tree, d):
    return [c for c in tree if tree[c] == d]


def deepest(tree, d, top):
    return max([trip(tree, d)] + [deepest(tree, c, top) for c in below(tree, d)]) - (trip(tree, d) if top else 0.0)


def far_first(tree, d):
    return sorted(below(tree, d), key=lambda c: (-max(deepest(tree, c, False), trip(tree, c)), -abs(c), c))


GATHER_TO = {d: far_first(GATHER_FROM, d) for d in DISTANCES}
GATHER_ORDER = [
    (own, d)
    for _, own, d in sorted(
        [(trip(GATHER_FROM, d), True, d) for d in DISTANCES if d != 0]
        + [(trip(GATHER_FROM, d) + Y_TRIP, False, d) for d in DISTANCES]
    )
]
SUM_TO = {d: below(SUM_FROM, d) for d in DISTANCES}
SUM_Y_ORDER = sorted(DISTANCES, key=lambda d: (-trip(SUM_FROM, d), d))


def sum_ready(d):
    at = Y_TRIP + SLOT * SUM_Y_ORDER.index(d)
    return max([at] + [sum_ready(c) + FIRST + EACH * abs(c - d) for c in SUM_TO[d]])


SUM_Z_ORDER = sorted(DISTANCES, key=lambda d: (d == 0, sum_ready(d)))
REACH = sorted(
    {s * (d - tree[d]) for tree in (GATHER_FROM, SUM_FROM) for d in tree for s in (1, -1)}
)


def nt(left, right):
    return lax.dot_general(left, right, (((1,), (1,)), ((), ())), preferred_element_type=F32)


def nn(left, right):
    return lax.dot_general(left, right, (((1,), (0,)), ((), ())), preferred_element_type=F32)


def tn(left, right):
    return lax.dot_general(left, right, (((0,), (0,)), ((), ())), preferred_element_type=F32)


def iota(shape, dim):
    return lax.broadcasted_iota(jnp.int32, shape, dim)


def one_hot(mask):
    return jnp.where(mask, 1.0, 0.0).astype(BF16)


def piece_to_block(i):
    return (i % 8) * 16 + (i // 16) * 2 + (i // 8) % 2


def slots_of(ids_ref, hid_at):
    taken = jnp.int32(0)
    slots = []
    for t in range(4):
        chosen = jnp.where(ids_ref[0, hid_at * 4 + t] * ids_ref[1, hid_at * 4 + t] == 0, 1, 0)
        slots.append(jnp.where(chosen == 1, taken, -1))
        taken = taken + chosen
    return slots


def kernel(
    x_hbm, h_hbm, wg_hbm, wu_hbm, ids_hbm, out_ref, wgrad_hbm,
    xs, hs, wg, wu, ids_a, ids_b, got, rows, hid, part, wgrad,
    mine, core_in, y_out, y_in, acc, z_out, z_in, s5, r5,
    load_sem, out_sem,
    got_r, gz_s, gy_s, gcore_s, c_s, c_r, y_s, y_r, z_s, z_r, pass_s, pass_r,
):
    sec = lax.axis_index("section")
    n_sec = lax.axis_size("section")
    me = lax.axis_index("hid")
    core = me % 2
    z = (me // 2) % Z
    y = me // (2 * Z)
    prev_sec = (sec + n_sec - 1) % n_sec
    next_sec = (sec + 1) % n_sec

    def hid_of(y_at, z_at, core_at):
        return (y_at * Z + z_at) * 2 + core_at

    other_y = hid_of(1 - y, z, core)
    other_core = hid_of(y, z, 1 - core)

    def along(d):
        return (z + d + Z) % Z

    def loads(src, dst, i):
        return pltpu.make_async_copy(src, dst, load_sem.at[i])

    def remote(src, dst, send, recv, to, section=None):
        return pltpu.make_async_remote_copy(
            src_ref=src, dst_ref=dst, send_sem=send, recv_sem=recv,
            device_id={"section": sec if section is None else section, "hid": to},
            device_id_type=MESH,
        )

    load_ids = loads(ids_hbm.at[sec], ids_a, 0)
    load_next = loads(ids_hbm.at[next_sec], ids_b, 1)
    load_x = loads(x_hbm.at[0], xs, 2)
    load_h = loads(h_hbm, hs, 3)
    load_wg = loads(wg_hbm, wg, 4)
    load_wu = loads(wu_hbm, wu, 5)
    for c in (load_ids, load_x, load_next, load_h, load_wg, load_wu):
        c.start()

    barrier = pltpu.get_barrier_semaphore()
    peers = [hid_of(y, along(d), core) for d in REACH] + [other_y, other_core]
    for p in peers:
        pl.semaphore_signal(barrier, inc=1, device_id={"section": sec, "hid": p}, device_id_type=MESH)
    pl.semaphore_signal(barrier, inc=1, device_id={"section": next_sec, "hid": me}, device_id_type=MESH)

    load_ids.wait()
    load_x.wait()
    slots = slots_of(ids_a, me)
    row, tok = iota((16, 4), 0), iota((16, 4), 1)
    slot_of_tok = jnp.full((16, 4), -1, jnp.int32)
    for t in range(4):
        slot_of_tok = jnp.where(tok == t, slots[t], slot_of_tok)
    tok_rows = xs[...]
    piece = jnp.zeros((16, CW), F32)
    for j in range(CH):
        pick = one_hot((row // 8 == slot_of_tok) & (row % 8 == j))
        piece += nn(pick, tok_rows[:, j * CW:(j + 1) * CW])
    got[core, z, y] = piece.astype(BF16)

    pl.semaphore_wait(barrier, len(peers) + 1)

    sends = []

    def send(*a, **k):
        c = remote(*a, **k)
        c.start()
        sends.append(c)

    def pass_on(core_at, d, y_at, sem, to):
        ref = got.at[core_at, along(-d), y_at]
        return remote(ref, ref, sem, got_r.at[core_at, along(-d), y_at], to)

    def landed(core_at, d, y_at):
        pass_on(core_at, d, y_at, gcore_s.at[0], other_core).wait_recv()

    def send_on(copy):
        copy.start()
        sends.append(copy)

    def own_side(d):
        for to in GATHER_TO[d]:
            send_on(pass_on(core, d, y, gz_s.at[to + Z // 2 - 1], hid_of(y, along(to - d), core)))
        i = d + Z // 2 - 1
        send_on(pass_on(core, d, y, gy_s.at[i], other_y))
        send_on(pass_on(core, d, y, gcore_s.at[i], other_core))

    def other_side(d):
        landed(core, d, 1 - y)
        send_on(pass_on(core, d, 1 - y, gcore_s.at[Z + d + Z // 2 - 1], other_core))

    own_side(0)

    load_h.wait()
    m, o = iota((128, 128), 0), iota((128, 128), 1)
    slot_at = ((m // 16) % 2) * 64 + ((m // 32) % 2) * 32 + ((m // 2) % 8) * 4 + (m // 64) * 2 + m % 2
    hid[...] = nt(one_hot(o == slot_at), hs[...])

    for is_own, d in GATHER_ORDER:
        if is_own:
            landed(core, d, y)
            own_side(d)
        else:
            other_side(d)

    to_block = one_hot(m == piece_to_block(o))

    def unpack(core_at):
        for o_z in range(2):
            for y_at in range(2):
                moved = nn(to_block, got[core_at, o_z * 8:o_z * 8 + 8, y_at].reshape(128, CW)).astype(BF16)
                b = (core_at * 2 + o_z) * 2 + y_at
                for j in range(CH):
                    rows[b, :, j * CW:(j + 1) * CW] = moved[j * 16:(j + 1) * 16]

    unpack(core)
    for d in DISTANCES:
        for y_at in range(2):
            landed(1 - core, d, y_at)
    unpack(1 - core)

    load_wg.wait()
    load_wu.wait()
    all_rows = rows[...].reshape(128, D)
    gate = nt(all_rows, wg[...])
    up = nt(all_rows, wu[...])
    sig = 1.0 / (1.0 + jnp.exp(-gate))
    hf = hid[...]
    d_gate = (hf * up * sig * (1.0 + gate * (1.0 - sig))).astype(BF16)
    d_up = (hf * gate * sig).astype(BF16)
    to_piece = one_hot(o == piece_to_block(m))
    part[...] = (nn(d_gate, wg[...]) + nn(d_up, wu[...])).astype(BF16).reshape(8, 16, D)

    def repack(core_at):
        for o_z in range(2):
            for y_at in range(2):
                own = part[(core_at * 2 + o_z) * 2 + y_at]
                stacked = jnp.concatenate([own[:, j * CW:(j + 1) * CW] for j in range(CH)], axis=0)
                moved = nn(to_piece, stacked).astype(BF16).reshape(8, 16, CW)
                mine[core_at, o_z * 8:o_z * 8 + 8, y_at] = moved

    def core_copy(i, d):
        return remote(mine.at[1 - core, along(-d)], core_in.at[i], c_s.at[i], c_r.at[i], other_core)

    def y_copy(i):
        return remote(y_out.at[i], y_in.at[i], y_s.at[i], y_r.at[i], other_y)

    def z_copy(d):
        i = d + Z // 2 - 1
        return remote(z_out.at[i], z_in.at[i], z_s.at[i], z_r.at[i], hid_of(y, along(SUM_FROM[d] - d), core))

    repack(1 - core)
    for i, d in enumerate(SUM_Y_ORDER):
        send_on(core_copy(i, d))
    repack(core)
    for i, d in enumerate(SUM_Y_ORDER):
        core_copy(i, d).wait_recv()
        at = along(-d)
        y_out[i] = (mine[core, at, 1 - y].astype(F32) + core_in[i, 1 - y].astype(F32)).astype(BF16)
        send_on(y_copy(i))
        acc[i] = mine[core, at, y].astype(F32) + core_in[i, y].astype(F32)
    for d in SUM_Z_ORDER:
        i = SUM_Y_ORDER.index(d)
        y_copy(i).wait_recv()
        total = acc[i] + y_in[i].astype(F32)
        for child in SUM_TO[d]:
            z_copy(child).wait_recv()
            total += z_in[child + Z // 2 - 1].astype(F32)
        if d != 0:
            z_out[d + Z // 2 - 1] = total.astype(BF16)
            send_on(z_copy(d))
    s5[...] = total.astype(BF16)
    send(s5, r5, pass_s, pass_r, me, section=prev_sec)

    for j in range(CH):
        cols = slice(j * CW, (j + 1) * CW)
        wgrad[:, cols] = tn(d_gate, rows[:, :, cols].reshape(128, CW)).astype(BF16)
    store = pltpu.make_async_copy(wgrad, wgrad_hbm, out_sem)
    store.start()
    load_next.wait()
    slots_n = slots_of(ids_b, me)
    trow, tcol = iota((4, 16), 0), iota((4, 16), 1)
    slot_of_row = jnp.full((4, 16), -1, jnp.int32)
    for t in range(4):
        slot_of_row = jnp.where(trow == t, slots_n[t], slot_of_row)
    store.wait()
    for c in sends[:-1]:
        c.wait_send()
    sends[-1].wait()
    last = r5[...]
    for j in range(CH):
        pick = one_hot((tcol // 8 == slot_of_row) & (tcol % 8 == j))
        out_ref[0, :, j * CW:(j + 1) * CW] = nn(pick, last).astype(BF16)


def per_device(layer_input, hidden_grad, gate_weight, up_weight, expert_ids):
    dma = pltpu.SemaphoreType.DMA
    anywhere = pl.BlockSpec(memory_space=pl.ANY)
    out, wgrad = pl.pallas_call(
        kernel,
        out_shape=(
            jax.ShapeDtypeStruct((1, 4, D), BF16),
            jax.ShapeDtypeStruct((FL, D), BF16),
        ),
        in_specs=[anywhere] * 5,
        out_specs=(pl.BlockSpec(memory_space=pltpu.VMEM), anywhere),
        scratch_shapes=[
            pltpu.VMEM((4, D), BF16),
            pltpu.VMEM((FL, 128), BF16),
            pltpu.VMEM((FL, D), BF16),
            pltpu.VMEM((FL, D), BF16),
            pltpu.SMEM((2, 256), jnp.int32),
            pltpu.SMEM((2, 256), jnp.int32),
            pltpu.VMEM((2, Z, 2, 16, CW), BF16),
            pltpu.VMEM((8, 16, D), BF16),
            pltpu.VMEM((128, FL), F32),
            pltpu.VMEM((8, 16, D), BF16),
            pltpu.VMEM((FL, D), BF16),
            pltpu.VMEM((2, Z, 2, 16, CW), BF16),
            pltpu.VMEM((16, 2, 16, CW), BF16),
            pltpu.VMEM((16, 16, CW), BF16),
            pltpu.VMEM((16, 16, CW), BF16),
            pltpu.VMEM((16, 16, CW), F32),
            pltpu.VMEM((Z, 16, CW), BF16),
            pltpu.VMEM((Z, 16, CW), BF16),
            pltpu.VMEM((16, CW), BF16),
            pltpu.VMEM((16, CW), BF16),
            dma((6,)),
            dma,
            dma((2, Z, 2)),
            dma((Z,)), dma((Z,)), dma((2 * Z,)),
            dma((Z,)), dma((Z,)),
            dma((Z,)), dma((Z,)),
            dma((Z,)), dma((Z,)),
            dma, dma,
        ],
        compiler_params=pltpu.CompilerParams(
            collective_id=0, has_side_effects=True, vmem_limit_bytes=60 * 2**20
        ),
        name="relay",
    )(
        layer_input,
        jnp.swapaxes(hidden_grad[0], 0, 1),
        jnp.swapaxes(gate_weight[0], 0, 1),
        jnp.swapaxes(up_weight[0], 0, 1),
        jnp.swapaxes(expert_ids, 1, 2),
    )
    return out, jnp.swapaxes(wgrad, 0, 1)[None]


def solution(mesh):
    return jax.shard_map(
        per_device,
        mesh=mesh,
        in_specs=(
            P("section", "hid", None),
            P("section", None, "hid"),
            P("section", None, "hid"),
            P("section", None, "hid"),
            P(),
        ),
        out_specs=(P("section", "hid", None), P("section", None, "hid")),
        check_vma=False,
    )
```

time: 70.2 us -> 62.5 us (0.89)
  the two profiles are of different devices: /device:TPU:18 before, /device:TPU:62 now
where the time goes in v2:
time: 62.5 us; the launch traced here: 62.2 us
  Pallas kernels  58 us (93%)
  local copies, waits for them, and re-layouts  3.55 us (6%)
  between operations  0.64 us (1%)
    pallas_call x1, Pallas kernels, per_device(): pl.pallas_call(kernel, out_shape=(jax.ShapeDtypeStruct((1, 4, D), BF16),...  58 us
    unnamed x2, local copies, waits for them, and re-layouts  3.55 us

profile of v2, /device:TPU:62, one launch (start us, length us, event | category | flops | bytes accessed | tf_op | source)
XLA Modules:
  0.0 62.2 jit_solution(9063944283968947434)
XLA Ops:
  0.6 58.0 %relay.1 = (bf16[1,4,4096]{2,1,0:T(4,128)(2,1)}, bf16[112,4096]{1,0:T(8,128)(2,1)}) custom-call(bf16[1,4,4096]{2,1,0:T(4,128)(2,1)} %x_hbm.1, bf16[112,128]{1,0:T(8,128)(2,1)} %bitcast.17, bf16[112,4096]{1,0:T(8,128)(2,1)} %bitcast.14, bf16[112,4096]{1,0:T(8,128)(2,1)} %bitcast.15, s32[16,2,256]{2,1,0:T(2,128)} %bitcast.16), custom_call_target="tpu_custom_call" | custom-call | tf_op jit(solution)/shard_map/relay/pallas_call | solution.py:307
  58.7 1.4 %copy.9 = bf16[1,4,4096]{2,1,0:T(4,128)(2,1)} copy(bf16[1,4,4096]{2,1,0:T(4,128)(2,1)} %get-tuple-element.8) | data formatting | bytes 65536
  60.0 2.2 %copy.10 = bf16[1,4096,112]{1,2,0:T(8,128)(2,1)} copy(bf16[1,4096,112]{1,2,0:T(8,128)(2,1)} %bitcast.13) | data formatting | bytes 1835008

commit v3 on v2

--- a/solution.py
+++ b/solution.py
@@ -15,6 +15,7 @@
 CH = 8
 CW = D // CH
 FL = 112
+PARTS = 7
 
 DISTANCES = tuple(range(1 - Z // 2, Z // 2 + 1))
 FIRST, EACH, Y_TRIP, SLOT = 1.4, 0.6, 2.1, 0.28
@@ -26,7 +27,7 @@
 
 
 GATHER_FROM = both_ways({1: 0, 2: 1, 3: 2, 4: 0, 5: 4, 6: 4, 7: 4, 8: 4})
-SUM_FROM = both_ways({1: 0, 2: 0, 3: 0, 4: 0, 5: 4, 6: 2, 7: 4, 8: 4})
+SUM_FROM = both_ways({1: 0, 2: 0, 3: 0, 4: 2, 5: 2, 6: 0, 7: 6, 8: 6})
 
 
 def trip(tree, d):
@@ -63,9 +64,7 @@
 
 
 SUM_Z_ORDER = sorted(DISTANCES, key=lambda d: (d == 0, sum_ready(d)))
-REACH = sorted(
-    {s * (d - tree[d]) for tree in (GATHER_FROM, SUM_FROM) for d in tree for s in (1, -1)}
-)
+REACH = sorted({s * (d - p) for d, p in GATHER_FROM.items() for s in (1, -1)})
 
 
 def nt(left, right):
@@ -103,9 +102,9 @@
 
 
 def kernel(
-    x_hbm, h_hbm, wg_hbm, wu_hbm, ids_hbm, out_ref, wgrad_hbm,
-    xs, hs, wg, wu, ids_a, ids_b, got, rows, hid, part, wgrad,
-    mine, core_in, y_out, y_in, acc, z_out, z_in, s5, r5,
+    x_hbm, h_hbm, wg_hbm, wu_hbm, ids_hbm, got_out, wgrad_hbm,
+    xs, hs, wg, wu, ids_a, got, rows, hid, part, wgrad,
+    mine, core_in, y_out, y_in, acc, z_out, z_in, s5,
     load_sem, out_sem,
     got_r, gz_s, gy_s, gcore_s, c_s, c_r, y_s, y_r, z_s, z_r, pass_s, pass_r,
 ):
@@ -138,12 +137,11 @@
         )
 
     load_ids = loads(ids_hbm.at[sec], ids_a, 0)
-    load_next = loads(ids_hbm.at[next_sec], ids_b, 1)
     load_x = loads(x_hbm.at[0], xs, 2)
     load_h = loads(h_hbm, hs, 3)
     load_wg = loads(wg_hbm, wg, 4)
     load_wu = loads(wu_hbm, wu, 5)
-    for c in (load_ids, load_x, load_next, load_h, load_wg, load_wu):
+    for c in (load_ids, load_x, load_h, load_wg, load_wu):
         c.start()
 
     barrier = pltpu.get_barrier_semaphore()
@@ -278,46 +276,73 @@
             z_out[d + Z // 2 - 1] = total.astype(BF16)
             send_on(z_copy(d))
     s5[...] = total.astype(BF16)
-    send(s5, r5, pass_s, pass_r, me, section=prev_sec)
+    send(s5, got_out, pass_s, pass_r, me, section=prev_sec)
 
     for j in range(CH):
         cols = slice(j * CW, (j + 1) * CW)
         wgrad[:, cols] = tn(d_gate, rows[:, :, cols].reshape(128, CW)).astype(BF16)
     store = pltpu.make_async_copy(wgrad, wgrad_hbm, out_sem)
     store.start()
-    load_next.wait()
-    slots_n = slots_of(ids_b, me)
-    trow, tcol = iota((4, 16), 0), iota((4, 16), 1)
-    slot_of_row = jnp.full((4, 16), -1, jnp.int32)
-    for t in range(4):
-        slot_of_row = jnp.where(trow == t, slots_n[t], slot_of_row)
     store.wait()
     for c in sends[:-1]:
         c.wait_send()
     sends[-1].wait()
-    last = r5[...]
+
+
+def finish(ids_hbm, got_hbm, wgrad_in, out_hbm, wgrad_out, ids, last_ref, tokens, held, sems, out_sems):
+    me = lax.axis_index("hid")
+    next_sec = (lax.axis_index("section") + 1) % lax.axis_size("section")
+    load = pltpu.make_async_copy(ids_hbm.at[next_sec], ids, sems.at[0])
+    load.start()
+    load_last = pltpu.make_async_copy(got_hbm, last_ref, sems.at[1 + PARTS])
+    load_last.start()
+    step = FL // PARTS
+    moves = []
+    for i in range(PARTS):
+        part = pl.ds(i * step, step)
+        moves.append((
+            pltpu.make_async_copy(wgrad_in.at[part], held.at[part], sems.at[1 + i]),
+            pltpu.make_async_copy(held.at[part], wgrad_out.at[part], out_sems.at[i]),
+        ))
+        moves[-1][0].start()
+    load.wait()
+    slots = slots_of(ids, me)
+    row, col = iota((4, 16), 0), iota((4, 16), 1)
+    slot_of_row = jnp.full((4, 16), -1, jnp.int32)
+    for t in range(4):
+        slot_of_row = jnp.where(row == t, slots[t], slot_of_row)
+    load_last.wait()
+    last = last_ref[...]
     for j in range(CH):
-        pick = one_hot((tcol // 8 == slot_of_row) & (tcol % 8 == j))
-        out_ref[0, :, j * CW:(j + 1) * CW] = nn(pick, last).astype(BF16)
+        pick = one_hot((col // 8 == slot_of_row) & (col % 8 == j))
+        tokens[:, j * CW:(j + 1) * CW] = nn(pick, last).astype(BF16)
+    store = pltpu.make_async_copy(tokens, out_hbm.at[0], out_sems.at[PARTS])
+    store.start()
+    for come, go in moves:
+        come.wait()
+        go.start()
+    for _, go in moves:
+        go.wait()
+    store.wait()
 
 
 def per_device(layer_input, hidden_grad, gate_weight, up_weight, expert_ids):
     dma = pltpu.SemaphoreType.DMA
     anywhere = pl.BlockSpec(memory_space=pl.ANY)
-    out, wgrad = pl.pallas_call(
+    ids = jnp.swapaxes(expert_ids, 1, 2)
+    sums, wgrad = pl.pallas_call(
         kernel,
         out_shape=(
-            jax.ShapeDtypeStruct((1, 4, D), BF16),
+            jax.ShapeDtypeStruct((16, CW), BF16),
             jax.ShapeDtypeStruct((FL, D), BF16),
         ),
         in_specs=[anywhere] * 5,
-        out_specs=(pl.BlockSpec(memory_space=pltpu.VMEM), anywhere),
+        out_specs=(anywhere, anywhere),
         scratch_shapes=[
             pltpu.VMEM((4, D), BF16),
             pltpu.VMEM((FL, 128), BF16),
             pltpu.VMEM((FL, D), BF16),
             pltpu.VMEM((FL, D), BF16),
-            pltpu.SMEM((2, 256), jnp.int32),
             pltpu.SMEM((2, 256), jnp.int32),
             pltpu.VMEM((2, Z, 2, 16, CW), BF16),
             pltpu.VMEM((8, 16, D), BF16),
@@ -331,7 +356,6 @@
             pltpu.VMEM((16, 16, CW), F32),
             pltpu.VMEM((Z, 16, CW), BF16),
             pltpu.VMEM((Z, 16, CW), BF16),
-            pltpu.VMEM((16, CW), BF16),
             pltpu.VMEM((16, CW), BF16),
             dma((6,)),
             dma,
@@ -351,8 +375,23 @@
         jnp.swapaxes(hidden_grad[0], 0, 1),
         jnp.swapaxes(gate_weight[0], 0, 1),
         jnp.swapaxes(up_weight[0], 0, 1),
-        jnp.swapaxes(expert_ids, 1, 2),
+        ids,
     )
+    out, wgrad = pl.pallas_call(
+        finish,
+        out_shape=(
+            jax.ShapeDtypeStruct((1, 4, D), BF16),
+            jax.ShapeDtypeStruct((FL, D), BF16),
+        ),
+        in_specs=[anywhere] * 3,
+        out_specs=(anywhere, anywhere),
+        scratch_shapes=[
+            pltpu.SMEM((2, 256), jnp.int32), pltpu.VMEM((16, CW), BF16), pltpu.VMEM((4, D), BF16),
+            pltpu.VMEM((FL, D), BF16), dma((2 + PARTS,)), dma((1 + PARTS,)),
+        ],
+        compiler_params=pltpu.CompilerParams(vmem_limit_bytes=60 * 2**20),
+        name="finish",
+    )(ids, sums, wgrad)
     return out, jnp.swapaxes(wgrad, 0, 1)[None]
 
 

time: 62.5 us -> 60 us (0.960)
  local copies, waits for them, and re-layouts: 3.55 us -> 0 us
  Pallas kernels: 58 us -> 59.2 us
    unnamed x2 -> x0, local copies, waits for them, and re-layouts: 3.55 us -> none
    pallas_call x1 -> x2, Pallas kernels: 58 us -> 59.2 us  [the longest x1 57.1 us: per_device(): pl.pallas_call(kernel, out_shape=(jax.ShapeDtypeStruct((16, CW), BF16), j...]
where the time goes in v3:
time: 60 us; the launch traced here: 59.8 us
  Pallas kernels  59.2 us (99%)
  between operations  0.64 us (1%)
    pallas_call x1, Pallas kernels, per_device(): pl.pallas_call(kernel, out_shape=(jax.ShapeDtypeStruct((16, CW), BF16), j...  57.1 us
    pallas_call x1, Pallas kernels, per_device(): pl.pallas_call(finish, out_shape=(jax.ShapeDtypeStruct((1, 4, D), BF16),...  2.08 us

profile of v3, /device:TPU:62, one launch (start us, length us, event | category | flops | bytes accessed | tf_op | source)
XLA Modules:
  0.0 59.8 jit_solution(826834916679519185)
XLA Ops:
  0.6 57.1 %relay.1 = (bf16[16,512]{1,0:T(8,128)(2,1)}, bf16[112,4096]{1,0:T(8,128)(2,1)}) custom-call(bf16[1,4,4096]{2,1,0:T(4,128)(2,1)} %x_hbm.1, bf16[112,128]{1,0:T(8,128)(2,1)} %bitcast.17, bf16[112,4096]{1,0:T(8,128)(2,1)} %bitcast.13, bf16[112,4096]{1,0:T(8,128)(2,1)} %bitcast.14, s32[16,2,256]{2,1,0:T(2,128)} %bitcast.15), custom_call_target="tpu_custom_call" | custom-call | tf_op jit(solution)/shard_map/relay/pallas_call | solution.py:333
  57.7 2.1 %finish.1 = (bf16[1,4,4096]{2,1,0:T(4,128)(2,1)}, bf16[112,4096]{1,0:T(8,128)(2,1)}) custom-call(s32[16,2,256]{2,1,0:T(2,128)} %bitcast.16, bf16[16,512]{1,0:T(8,128)(2,1)} %get-tuple-element.6.got_hbm, bf16[112,4096]{1,0:T(8,128)(2,1)} %get-tuple-element.7.wgrad_in), custom_call_target="tpu_custom_call" | custom-call | tf_op jit(solution)/shard_map/finish/pallas_call | solution.py:380

commit v4 on v3

--- a/solution.py
+++ b/solution.py
@@ -26,7 +26,7 @@
     return {**tree, **back}
 
 
-GATHER_FROM = both_ways({1: 0, 2: 1, 3: 2, 4: 0, 5: 4, 6: 4, 7: 4, 8: 4})
+GATHER_FROM = both_ways({1: 0, 2: 1, 3: 4, 4: 0, 5: 4, 6: 4, 7: 4, 8: 4})
 SUM_FROM = both_ways({1: 0, 2: 0, 3: 0, 4: 2, 5: 2, 6: 0, 7: 6, 8: 6})
 
 
@@ -64,6 +64,7 @@
 
 
 SUM_Z_ORDER = sorted(DISTANCES, key=lambda d: (d == 0, sum_ready(d)))
+LAST_ORDER = [d for d in SUM_Z_ORDER if SUM_FROM.get(d, 0) == 0]
 REACH = sorted({s * (d - p) for d, p in GATHER_FROM.items() for s in (1, -1)})
 
 
@@ -106,7 +107,7 @@
     xs, hs, wg, wu, ids_a, got, rows, hid, part, wgrad,
     mine, core_in, y_out, y_in, acc, z_out, z_in, s5,
     load_sem, out_sem,
-    got_r, gz_s, gy_s, gcore_s, c_s, c_r, y_s, y_r, z_s, z_r, pass_s, pass_r,
+    got_r, gz_s, gy_s, gcore_s, c_s, c_r, y_s, y_r, z_s, z_r, give_sem, column_in,
 ):
     sec = lax.axis_index("section")
     n_sec = lax.axis_size("section")
@@ -148,7 +149,7 @@
     peers = [hid_of(y, along(d), core) for d in REACH] + [other_y, other_core]
     for p in peers:
         pl.semaphore_signal(barrier, inc=1, device_id={"section": sec, "hid": p}, device_id_type=MESH)
-    pl.semaphore_signal(barrier, inc=1, device_id={"section": next_sec, "hid": me}, device_id_type=MESH)
+    pl.semaphore_signal(barrier, inc=1, device_id={"section": prev_sec, "hid": me}, device_id_type=MESH)
 
     load_ids.wait()
     load_x.wait()
@@ -209,6 +210,7 @@
         else:
             other_side(d)
 
+    pl.semaphore_signal(column_in, inc=1, device_id={"section": next_sec, "hid": me}, device_id_type=MESH)
     to_block = one_hot(m == piece_to_block(o))
 
     def unpack(core_at):
@@ -253,7 +255,9 @@
 
     def z_copy(d):
         i = d + Z // 2 - 1
-        return remote(z_out.at[i], z_in.at[i], z_s.at[i], z_r.at[i], hid_of(y, along(SUM_FROM[d] - d), core))
+        up = SUM_FROM.get(d, 0)
+        section = prev_sec if up == 0 else sec
+        return remote(z_out.at[i], z_in.at[i], z_s.at[i], z_r.at[i], hid_of(y, along(up - d), core), section)
 
     repack(1 - core)
     for i, d in enumerate(SUM_Y_ORDER):
@@ -265,28 +269,37 @@
         y_out[i] = (mine[core, at, 1 - y].astype(F32) + core_in[i, 1 - y].astype(F32)).astype(BF16)
         send_on(y_copy(i))
         acc[i] = mine[core, at, y].astype(F32) + core_in[i, y].astype(F32)
+    told = False
     for d in SUM_Z_ORDER:
         i = SUM_Y_ORDER.index(d)
         y_copy(i).wait_recv()
         total = acc[i] + y_in[i].astype(F32)
-        for child in SUM_TO[d]:
-            z_copy(child).wait_recv()
-            total += z_in[child + Z // 2 - 1].astype(F32)
         if d != 0:
-            z_out[d + Z // 2 - 1] = total.astype(BF16)
-            send_on(z_copy(d))
-    s5[...] = total.astype(BF16)
-    send(s5, got_out, pass_s, pass_r, me, section=prev_sec)
+            for child in SUM_TO[d]:
+                z_copy(child).wait_recv()
+                total += z_in[child + Z // 2 - 1].astype(F32)
+        if SUM_FROM.get(d, 0) == 0 and not told:
+            pl.semaphore_wait(column_in, 1)
+            told = True
+        z_out[d + Z // 2 - 1] = total.astype(BF16)
+        send_on(z_copy(d))
 
     for j in range(CH):
         cols = slice(j * CW, (j + 1) * CW)
         wgrad[:, cols] = tn(d_gate, rows[:, :, cols].reshape(128, CW)).astype(BF16)
     store = pltpu.make_async_copy(wgrad, wgrad_hbm, out_sem)
     store.start()
+    total = jnp.zeros((16, CW), F32)
+    for child in LAST_ORDER:
+        z_copy(child).wait_recv()
+        total += z_in[child + Z // 2 - 1].astype(F32)
+    s5[...] = total.astype(BF16)
+    give = pltpu.make_async_copy(s5, got_out, give_sem)
+    give.start()
     store.wait()
-    for c in sends[:-1]:
+    for c in sends:
         c.wait_send()
-    sends[-1].wait()
+    give.wait()
 
 
 def finish(ids_hbm, got_hbm, wgrad_in, out_hbm, wgrad_out, ids, last_ref, tokens, held, sems, out_sems):
@@ -364,7 +377,7 @@
             dma((Z,)), dma((Z,)),
             dma((Z,)), dma((Z,)),
             dma((Z,)), dma((Z,)),
-            dma, dma,
+            dma, pltpu.SemaphoreType.REGULAR,
         ],
         compiler_params=pltpu.CompilerParams(
             collective_id=0, has_side_effects=True, vmem_limit_bytes=60 * 2**20

time: 60 us -> 58.2 us (0.970)
  the two profiles are of different devices: /device:TPU:62 before, /device:TPU:16 now
where the time goes in v4:
time: 58.2 us; the launch traced here: 58 us
  Pallas kernels  57.4 us (99%)
  between operations  0.64 us (1%)
    pallas_call x1, Pallas kernels, per_device(): pl.pallas_call(kernel, out_shape=(jax.ShapeDtypeStruct((16, CW), BF16), j...  55.3 us
    pallas_call x1, Pallas kernels, per_device(): pl.pallas_call(finish, out_shape=(jax.ShapeDtypeStruct((1, 4, D), BF16),...  2.08 us

profile of v4, /device:TPU:16, one launch (start us, length us, event | category | flops | bytes accessed | tf_op | source)
XLA Modules:
  0.0 58.0 jit_solution(14610386286384089966)
XLA Ops:
  0.6 55.3 %relay.1 = (bf16[16,512]{1,0:T(8,128)(2,1)}, bf16[112,4096]{1,0:T(8,128)(2,1)}) custom-call(bf16[1,4,4096]{2,1,0:T(4,128)(2,1)} %x_hbm.1, bf16[112,128]{1,0:T(8,128)(2,1)} %bitcast.17, bf16[112,4096]{1,0:T(8,128)(2,1)} %bitcast.13, bf16[112,4096]{1,0:T(8,128)(2,1)} %bitcast.14, s32[16,2,256]{2,1,0:T(2,128)} %bitcast.15), custom_call_target="tpu_custom_call" | custom-call | tf_op jit(solution)/shard_map/relay/pallas_call | solution.py:346
  55.9 2.1 %finish.1 = (bf16[1,4,4096]{2,1,0:T(4,128)(2,1)}, bf16[112,4096]{1,0:T(8,128)(2,1)}) custom-call(s32[16,2,256]{2,1,0:T(2,128)} %bitcast.16, bf16[16,512]{1,0:T(8,128)(2,1)} %get-tuple-element.6.got_hbm, bf16[112,4096]{1,0:T(8,128)(2,1)} %get-tuple-element.7.wgrad_in), custom_call_target="tpu_custom_call" | custom-call | tf_op jit(solution)/shard_map/finish/pallas_call | solution.py:393

commit v5 on v4

--- a/solution.py
+++ b/solution.py
@@ -18,7 +18,7 @@
 PARTS = 7
 
 DISTANCES = tuple(range(1 - Z // 2, Z // 2 + 1))
-FIRST, EACH, Y_TRIP, SLOT = 1.4, 0.6, 2.1, 0.28
+FIRST, EACH, Y_TRIP, SLOT = 1.4, 0.6, 3.0, 0.28
 
 
 def both_ways(tree):
@@ -289,6 +289,8 @@
         wgrad[:, cols] = tn(d_gate, rows[:, :, cols].reshape(128, CW)).astype(BF16)
     store = pltpu.make_async_copy(wgrad, wgrad_hbm, out_sem)
     store.start()
+    for c in sends:
+        c.wait_send()
     total = jnp.zeros((16, CW), F32)
     for child in LAST_ORDER:
         z_copy(child).wait_recv()
@@ -297,8 +299,6 @@
     give = pltpu.make_async_copy(s5, got_out, give_sem)
     give.start()
     store.wait()
-    for c in sends:
-        c.wait_send()
     give.wait()
 
 

time: 58.2 us -> 58.6 us (level)
  no operation moved by 1% of the time
where the time goes in v5:
time: 58.6 us; the launch traced here: 58.4 us
  Pallas kernels  57.8 us (99%)
  between operations  0.64 us (1%)
    pallas_call x1, Pallas kernels, per_device(): pl.pallas_call(kernel, out_shape=(jax.ShapeDtypeStruct((16, CW), BF16), j...  55.7 us
    pallas_call x1, Pallas kernels, per_device(): pl.pallas_call(finish, out_shape=(jax.ShapeDtypeStruct((1, 4, D), BF16),...  2.08 us

profile of v5, /device:TPU:16, one launch (start us, length us, event | category | flops | bytes accessed | tf_op | source)
XLA Modules:
  0.0 58.4 jit_solution(12373594061098083320)
XLA Ops:
  0.6 55.7 %relay.1 = (bf16[16,512]{1,0:T(8,128)(2,1)}, bf16[112,4096]{1,0:T(8,128)(2,1)}) custom-call(bf16[1,4,4096]{2,1,0:T(4,128)(2,1)} %x_hbm.1, bf16[112,128]{1,0:T(8,128)(2,1)} %bitcast.17, bf16[112,4096]{1,0:T(8,128)(2,1)} %bitcast.13, bf16[112,4096]{1,0:T(8,128)(2,1)} %bitcast.14, s32[16,2,256]{2,1,0:T(2,128)} %bitcast.15), custom_call_target="tpu_custom_call" | custom-call | tf_op jit(solution)/shard_map/relay/pallas_call | solution.py:346
  56.3 2.1 %finish.1 = (bf16[1,4,4096]{2,1,0:T(4,128)(2,1)}, bf16[112,4096]{1,0:T(8,128)(2,1)}) custom-call(s32[16,2,256]{2,1,0:T(2,128)} %bitcast.16, bf16[16,512]{1,0:T(8,128)(2,1)} %get-tuple-element.6.got_hbm, bf16[112,4096]{1,0:T(8,128)(2,1)} %get-tuple-element.7.wgrad_in), custom_call_target="tpu_custom_call" | custom-call | tf_op jit(solution)/shard_map/finish/pallas_call | solution.py:393
